TPU v7x, 32 devices: a whole 2x2x4 slice. The times are simulated.
32 devices in a mesh: shots: 2 (over y), wide: 16 (over z, x, core).
Axes of the slice: x: 2, y: 2, z: 4, core: 2. Of those that a mesh axis runs over, the one named last changes fastest.
Arguments:
- src_now: float32 [32, 64, 128], P('wide', 'shots'), parts along dimension 1, may hold values from -6 to 6
- src_old: float32 [32, 64, 128], P('wide', 'shots'), parts along dimension 1, may hold values from -6 to 6
- rcv_now: float32 [32, 256, 32], P('wide', 'shots'), parts along dimension 1, may hold values from -6 to 6
- rcv_old: float32 [32, 256, 32], P('wide', 'shots'), parts along dimension 1, may hold values from -6 to 6
- medium: float32 [3, 32, 128, 32], P(None, 'wide'), may hold values from 0.04 to 0.24
- wavelet: float32 [4], replicated, may hold values from -4 to 4
- shot: int32 [6], P('shots'), parts along dimension 0, may hold values from 0 to 31
- traces: float32 [32, 128, 4], P('wide', 'shots'), parts along dimension 1, may hold values from -6 to 6
- rec_x: int32 [32, 128], P('wide', 'shots'), parts along dimension 1, may hold values from 0 to 31
- lag_order: int32 [33], replicated, may hold values from 0 to 32, each once
Outputs:
- src_next: float32 [32, 64, 128], P('wide', 'shots'), parts along dimension 1
- src_prior: float32 [32, 64, 128], P('wide', 'shots'), parts along dimension 1
- rcv_next: float32 [32, 256, 32], P('wide', 'shots'), parts along dimension 1
- rcv_prior: float32 [32, 256, 32], P('wide', 'shots'), parts along dimension 1
- image: float32 [66, 32, 128, 32], P('shots', 'wide'), parts along dimension 0
There are 2 independent parts, one for each index of `shots`. A program takes and returns all parts, laid end to end along the dimension named above; an argument that names none is the same for every part. Nothing has to cross between parts.
Inputs may be any that keep to these rules, and one draw needn't show every extreme that they name: `lag_order`: each of the 33 lag slots once.
All inputs are finite; a program needn't handle non-finite values.
Results may differ from a plain program's by a relative error of at most 0.0003.
Values sent between devices are 32-bit elements; how exact they have to be, the bound alone decides.
A program may use at most 64 MiB of HBM per device.

v0:
```python
import jax
import jax.numpy as jnp
from jax import lax
from jax.sharding import PartitionSpec as P


def extended(array, sides, width):
    for axis, dim in sides:
        devices, length = (lax.axis_size(axis), array.shape[dim])
        up = [(i, (i + 1) % devices) for i in range(devices - 1)]
        down = [(j, i) for i, j in up]
        last = lax.slice_in_dim(array, length - width, length, axis=dim)
        initial = lax.slice_in_dim(array, 0, width, axis=dim)
        before = lax.ppermute(last, axis, up)
        after = lax.ppermute(initial, axis, down)
        array = jnp.concatenate([before, array, after], axis=dim)
    return array


def window_sum(padded, dim, count):

    def window_at(start):
        return lax.slice_in_dim(padded, start, start + count, axis=dim)

    return (
        -1.0 / 12.0 * (window_at(0) + window_at(4))
        + 4.0 / 3.0 * (window_at(1) + window_at(3))
        - 2.5 * window_at(2)
    )


def widen(field, dim):
    widths = [(0, 0)] * field.ndim
    widths[dim] = (2, 2)
    return jnp.pad(field, widths)


def second(field, dim):
    return window_sum(widen(field, dim), dim, field.shape[dim])


def lagged(snaps, lag_order):
    half = (lag_order.shape[0] - 1) // 2
    cells_x = snaps[0][0].shape[2]
    widths = ((0, 0), (0, 0), (half, half))
    padded = [(jnp.pad(source, widths), jnp.pad(receiver, widths)) for source, receiver in snaps]

    def one_plane(slot):
        offset = slot - half
        total = None
        for source, receiver in padded:
            moved_src = lax.dynamic_slice_in_dim(source, half - offset, cells_x, 2)
            moved_rcv = lax.dynamic_slice_in_dim(receiver, half + offset, cells_x, 2)
            product = moved_src * moved_rcv
            total = product if total is None else total + product
        return total

    return lax.map(one_plane, lag_order)


def indicator(count, first, target):
    return (jnp.arange(count, dtype=jnp.int32) + first == target).astype(jnp.float32)


def on_device(src_now, src_old, rcv_now, rcv_old, medium, wavelet, shot, traces, rec_x, lag_order):
    slab_x, cells_y, cells_z = src_now.shape
    slab_y, _, cells_x = rcv_now.shape
    device = lax.axis_index("wide")
    steps = wavelet.shape[0]
    onehot = (rec_x[:, :, None] == jnp.arange(cells_x, dtype=jnp.int32)[None, None, :]).astype(
        jnp.float32
    )
    shot_rcv = (
        indicator(slab_y, device * slab_y, shot[1])[:, None, None]
        * indicator(cells_z, 0, shot[2])[None, :, None]
        * indicator(cells_x, 0, shot[0])[None, None, :]
    )
    snaps = []
    turned_now, turned_old = (
        lax.all_to_all(src_now, "wide", split_axis=1, concat_axis=0, tiled=True),
        lax.all_to_all(src_old, "wide", split_axis=1, concat_axis=0, tiled=True),
    )
    pair_now = jnp.stack([jnp.transpose(turned_now, (1, 2, 0)), rcv_now])
    pair_old = jnp.stack([jnp.transpose(turned_old, (1, 2, 0)), rcv_old])
    for step in range(steps):
        widened = extended(pair_now, (("wide", 1),), 2)
        spread = (
            medium[0] * second(pair_now, 3)
            + medium[1] * window_sum(widened, 1, slab_y)
            + medium[2] * second(pair_now, 2)
        )
        pair_new = 2.0 * pair_now - pair_old + spread
        pair_new = pair_new.at[0].add(-wavelet[step] * shot_rcv)
        pair_new = pair_new.at[1, :, 0, :].add(
            jnp.einsum("yr,yrx->yx", traces[:, :, step], onehot, precision=lax.Precision.HIGHEST)
        )
        pair_old, pair_now = (pair_now, pair_new)
        if step % 2 == 1:
            snaps.append((pair_now[0], pair_now[1]))
    back_now, back_old = (
        lax.all_to_all(pair_now[0], "wide", split_axis=2, concat_axis=0, tiled=True),
        lax.all_to_all(pair_old[0], "wide", split_axis=2, concat_axis=0, tiled=True),
    )
    src_next = jnp.transpose(back_now, (2, 0, 1))
    src_prior = jnp.transpose(back_old, (2, 0, 1))
    return (src_next, src_prior, pair_now[1], pair_old[1], lagged(snaps, lag_order))


def solution(mesh):
    return jax.shard_map(
        on_device,
        mesh=mesh,
        in_specs=(
            P("wide", "shots", None),
            P("wide", "shots", None),
            P("wide", "shots", None),
            P("wide", "shots", None),
            P(None, "wide", None, None),
            P(),
            P("shots"),
            P("wide", "shots", None),
            P("wide", "shots"),
            P(),
        ),
        out_specs=(
            P("wide", "shots", None),
            P("wide", "shots", None),
            P("wide", "shots", None),
            P("wide", "shots", None),
            P("shots", "wide", None, None),
        ),
        check_vma=False,
    )
```

profile of v0, /device:TPU:0, one launch (start us, length us, event | category | flops | bytes accessed | tf_op | source)
XLA Modules:
  0.0 220.2 jit_solution(10086139652803222354)
XLA Ops:
  0.7 1.4 copy.55
  2.1 7.4 %all-to-all-start = ((f32[2,32,128]{2,0,1:T(2,128)}), f32[2,32,128]{2,0,1:T(2,128)S(1)}, u32[]{:S(2)}, u32[]{:S(2)}) async-start(f32[2,32,128]{2,0,1:T(2,128)} %copy.55), calls=%async_computation | async-start | bytes 65536 | tf_op jit(solution)/shard_map/all_to_all | solution.py:80
  9.5 0.8 slice_bitcast_fusion.8
  10.3 1.4 copy.57
  11.7 1.4 fusion.109
  13.0 0.6 compare_convert_fusion.1
  13.7 0.7 compare_convert_fusion.2
  14.4 1.4 fusion.108
  16.5 6.0 %all-to-all-start.1 = ((f32[2,32,128]{2,0,1:T(2,128)}), f32[2,32,128]{2,0,1:T(2,128)S(1)}, u32[]{:S(2)}, u32[]{:S(2)}) async-start(f32[2,32,128]{2,0,1:T(2,128)} %copy.57), calls=%async_computation.1 | async-start | bytes 65536 | tf_op jit(solution)/shard_map/all_to_all | solution.py:81
  22.5 0.8 pad_maximum_fusion.10
  23.3 2.3 %collective-permute-start = (f32[2,2,128,32]{2,3,1,0:T(8,128)S(1)}, f32[2,2,128,32]{2,3,1,0:T(8,128)S(1)}, u32[]{:S(2)}, u32[]{:S(2)}) collective-permute-start(f32[2,2,128,32]{2,3,1,0:T(8,128)S(1)} %pad_maximum_fusion.10), channel_id=1, source_target_pairs={{0,1},{1,2},{2,3},{3,4},{4,5},{5,6},{6,7},{7,8},{8,9},{9,10},{10,1... | collective-permute-start | bytes 196616 | tf_op jit(solution)/shard_map/ppermute | solution.py:14
  25.6 1.3 collective-permute-start.1
  26.9 0.7 compare_convert_fusion
  27.5 1.6 all-to-all-done.1
  29.1 0.7 collective-permute-done.1
  29.9 0.9 fusion.11
  31.3 4.8 %collective-permute-start.2 = (f32[2,2,128,32]{2,3,1,0:T(8,128)S(1)}, f32[2,2,128,32]{2,3,1,0:T(8,128)S(1)}, u32[]{:S(2)}, u32[]{:S(2)}) collective-permute-start(f32[2,2,128,32]{2,3,1,0:T(8,128)S(1)} %scatter-add.29), channel_id=1, source_target_pairs={{0,1},{1,2},{2,3},{3,4},{4,5},{5,6},{6,7},{7,8},{8,9},{9,10},{10,1... | collective-permute-start | bytes 196616 | tf_op jit(solution)/shard_map/ppermute | solution.py:14
  36.2 1.3 collective-permute-start.3
  38.1 1.2 collective-permute-done.3
  40.0 5.1 %collective-permute-start.4 = (f32[2,2,128,32]{2,3,1,0:T(8,128)S(1)}, f32[2,2,128,32]{2,3,1,0:T(8,128)S(1)}, u32[]{:S(2)}, u32[]{:S(2)}) collective-permute-start(f32[2,2,128,32]{2,3,1,0:T(8,128)S(1)} %scatter-add.31), channel_id=1, source_target_pairs={{0,1},{1,2},{2,3},{3,4},{4,5},{5,6},{6,7},{7,8},{8,9},{9,10},{10,1... | collective-permute-start | bytes 196616 | tf_op jit(solution)/shard_map/ppermute | solution.py:14
  45.1 1.3 collective-permute-start.5
  48.9 5.3 %collective-permute-start.6 = (f32[2,2,128,32]{2,3,1,0:T(8,128)S(1)}, f32[2,2,128,32]{2,3,1,0:T(8,128)S(1)}, u32[]{:S(2)}, u32[]{:S(2)}) collective-permute-start(f32[2,2,128,32]{2,3,1,0:T(8,128)S(1)} %scatter-add.35), channel_id=1, source_target_pairs={{0,1},{1,2},{2,3},{3,4},{4,5},{5,6},{6,7},{7,8},{8,9},{9,10},{10,1... | collective-permute-start | bytes 196616 | tf_op jit(solution)/shard_map/ppermute | solution.py:14
  54.1 1.3 collective-permute-start.7
  56.1 0.6 copy.66
  56.7 7.4 %all-to-all-start.3 = ((f32[2,128,32]{1,0,2:T(2,128)}), f32[2,128,32]{1,0,2:T(2,128)S(1)}, u32[]{:S(2)}, u32[]{:S(2)}) async-start(f32[2,128,32]{1,0,2:T(2,128)} %copy.66), calls=%async_computation.3 | async-start | bytes 65536 | tf_op jit(solution)/shard_map/all_to_all | solution.py:102
  64.2 6.6 %all-to-all-done.3 = f32[2,128,32]{1,0,2:T(2,128)S(1)} async-done(((f32[2,128,32]{1,0,2:T(2,128)}), f32[2,128,32]{1,0,2:T(2,128)S(1)}, u32[]{:S(2)}, u32[]{:S(2)}) %all-to-all-start.3) | async-done | bytes 32800 | tf_op jit(solution)/shard_map/all_to_all | solution.py:102
  70.8 0.6 copy.68
  72.1 0.6 copy.63
  72.8 3.5 %all-to-all-start.2 = ((f32[2,128,32]{1,0,2:T(2,128)}), f32[2,128,32]{1,0,2:T(2,128)S(1)}, u32[]{:S(2)}, u32[]{:S(2)}) async-start(f32[2,128,32]{1,0,2:T(2,128)} %copy.63), calls=%async_computation.2 | async-start | bytes 65536 | tf_op jit(solution)/shard_map/all_to_all | solution.py:101
  76.3 143.2 %while.23 = (s32[]{:T(128)}, f32[33,2,128,32]{2,3,1,0:T(8,128)}, s32[33]{0:T(128)S(1)}, f32[2,128,64]{1,2,0:T(8,128)S(1)}, f32[2,128,64]{1,2,0:T(8,128)S(1)}, /*...) while((s32[]{:T(128)}, f32[33,2,128,32]{2,3,1,0:T(8,128)}, ...), condition=%wide.region_1.2_spmd, body=%wide.region_0.1_spmd.sunk | while | flops 24586 | bytes 819957 | solution.py:58
  80.0 0.6 constant_dynamic-update-slice_fusion.2
  84.3 0.6 constant_dynamic-update-slice_fusion.2
  88.7 0.6 constant_dynamic-update-slice_fusion.2
  93.0 0.6 constant_dynamic-update-slice_fusion.2
  97.4 0.6 constant_dynamic-update-slice_fusion.2
  101.7 0.6 constant_dynamic-update-slice_fusion.2
  106.0 0.6 constant_dynamic-update-slice_fusion.2
  110.4 0.6 constant_dynamic-update-slice_fusion.2
  114.7 0.6 constant_dynamic-update-slice_fusion.2
  123.4 0.6 constant_dynamic-update-slice_fusion.2
  127.7 0.6 constant_dynamic-update-slice_fusion.2
  136.4 0.6 constant_dynamic-update-slice_fusion.2
  140.8 0.6 constant_dynamic-update-slice_fusion.2
  145.1 0.6 constant_dynamic-update-slice_fusion.2
  149.4 0.6 constant_dynamic-update-slice_fusion.2
  153.8 0.6 constant_dynamic-update-slice_fusion.2
  158.1 0.6 constant_dynamic-update-slice_fusion.2
  219.5 0.6 copy.65
  (359 shorter events, 51.2 us)
Async XLA Ops:
  0.6 38.7 %copy-start = (f32[2,128,32]{1,2,0:T(8,128)S(1)}, f32[2,128,32]{1,2,0:T(8,128)}, u32[]{:S(2)}) copy-start(f32[2,128,32]{1,2,0:T(8,128)} %param.30) | copy-start | bytes 98308
  0.6 30.2 %copy-start.2 = (f32[2,64,4]{1,2,0:T(4,128)S(1)}, f32[2,64,4]{1,2,0:T(4,128)}, u32[]{:S(2)}) copy-start(f32[2,64,4]{1,2,0:T(4,128)} %param.35) | copy-start | bytes 6148
  0.7 30.2 %copy-start.3 = (s32[2,64]{1,0:T(2,128)S(1)}, s32[2,64]{1,0:T(2,128)}, u32[]{:S(2)}) copy-start(s32[2,64]{1,0:T(2,128)} %param.36) | copy-start | bytes 1540
  2.1 14.4 %all-to-all-start = ((f32[2,32,128]{2,0,1:T(2,128)}), f32[2,32,128]{2,0,1:T(2,128)S(1)}, u32[]{:S(2)}, u32[]{:S(2)}) async-start(f32[2,32,128]{2,0,1:T(2,128)} %copy.55), calls=%async_computation | async-start | bytes 65536 | tf_op jit(solution)/shard_map/all_to_all | solution.py:80
  16.5 12.7 %all-to-all-start.1 = ((f32[2,32,128]{2,0,1:T(2,128)}), f32[2,32,128]{2,0,1:T(2,128)S(1)}, u32[]{:S(2)}, u32[]{:S(2)}) async-start(f32[2,32,128]{2,0,1:T(2,128)} %copy.57), calls=%async_computation.1 | async-start | bytes 65536 | tf_op jit(solution)/shard_map/all_to_all | solution.py:81
  23.3 5.9 %collective-permute-start = (f32[2,2,128,32]{2,3,1,0:T(8,128)S(1)}, f32[2,2,128,32]{2,3,1,0:T(8,128)S(1)}, u32[]{:S(2)}, u32[]{:S(2)}) collective-permute-start(f32[2,2,128,32]{2,3,1,0:T(8,128)S(1)} %pad_maximum_fusion.10), channel_id=1, source_target_pairs={{0,1},{1,2},{2,3},{3,4},{4,5},{5,6},{6,7},{7,8},{8,9},{9,10},{10,1... | collective-permute-start | bytes 196616 | tf_op jit(solution)/shard_map/ppermute | solution.py:14
  25.6 4.3 %collective-permute-start.1 = (f32[2,2,128,32]{2,3,1,0:T(8,128)S(1)}, f32[2,2,128,32]{2,3,1,0:T(8,128)S(1)}, u32[]{:S(2)}, u32[]{:S(2)}) collective-permute-start(f32[2,2,128,32]{2,3,1,0:T(8,128)S(1)} %pad_maximum_fusion.10), channel_id=1, source_target_pairs={{1,0},{2,1},{3,2},{4,3},{5,4},{6,5},{7,6},{8,7},{9,8},{10,9},{11,1... | collective-permute-start | bytes 196616 | tf_op jit(solution)/shard_map/ppermute | solution.py:15
  31.3 6.8 %collective-permute-start.2 = (f32[2,2,128,32]{2,3,1,0:T(8,128)S(1)}, f32[2,2,128,32]{2,3,1,0:T(8,128)S(1)}, u32[]{:S(2)}, u32[]{:S(2)}) collective-permute-start(f32[2,2,128,32]{2,3,1,0:T(8,128)S(1)} %scatter-add.29), channel_id=1, source_target_pairs={{0,1},{1,2},{2,3},{3,4},{4,5},{5,6},{6,7},{7,8},{8,9},{9,10},{10,1... | collective-permute-start | bytes 196616 | tf_op jit(solution)/shard_map/ppermute | solution.py:14
  36.2 3.1 %collective-permute-start.3 = (f32[2,2,128,32]{2,3,1,0:T(8,128)S(1)}, f32[2,2,128,32]{2,3,1,0:T(8,128)S(1)}, u32[]{:S(2)}, u32[]{:S(2)}) collective-permute-start(f32[2,2,128,32]{2,3,1,0:T(8,128)S(1)} %scatter-add.29), channel_id=1, source_target_pairs={{1,0},{2,1},{3,2},{4,3},{5,4},{6,5},{7,6},{8,7},{9,8},{10,9},{11,1... | collective-permute-start | bytes 196616 | tf_op jit(solution)/shard_map/ppermute | solution.py:15
  40.0 7.7 %collective-permute-start.4 = (f32[2,2,128,32]{2,3,1,0:T(8,128)S(1)}, f32[2,2,128,32]{2,3,1,0:T(8,128)S(1)}, u32[]{:S(2)}, u32[]{:S(2)}) collective-permute-start(f32[2,2,128,32]{2,3,1,0:T(8,128)S(1)} %scatter-add.31), channel_id=1, source_target_pairs={{0,1},{1,2},{2,3},{3,4},{4,5},{5,6},{6,7},{7,8},{8,9},{9,10},{10,1... | collective-permute-start | bytes 196616 | tf_op jit(solution)/shard_map/ppermute | solution.py:14
  45.1 3.1 %collective-permute-start.5 = (f32[2,2,128,32]{2,3,1,0:T(8,128)S(1)}, f32[2,2,128,32]{2,3,1,0:T(8,128)S(1)}, u32[]{:S(2)}, u32[]{:S(2)}) collective-permute-start(f32[2,2,128,32]{2,3,1,0:T(8,128)S(1)} %scatter-add.31), channel_id=1, source_target_pairs={{1,0},{2,1},{3,2},{4,3},{5,4},{6,5},{7,6},{8,7},{9,8},{10,9},{11,1... | collective-permute-start | bytes 196616 | tf_op jit(solution)/shard_map/ppermute | solution.py:15
  48.4 27.9 %copy-start.4 = (s32[33]{0:T(128)S(1)}, s32[33]{0:T(128)}, u32[]{:S(2)}) copy-start(s32[33]{0:T(128)} %param.37) | copy-start | bytes 400
  48.9 22.5 %collective-permute-start.6 = (f32[2,2,128,32]{2,3,1,0:T(8,128)S(1)}, f32[2,2,128,32]{2,3,1,0:T(8,128)S(1)}, u32[]{:S(2)}, u32[]{:S(2)}) collective-permute-start(f32[2,2,128,32]{2,3,1,0:T(8,128)S(1)} %scatter-add.35), channel_id=1, source_target_pairs={{0,1},{1,2},{2,3},{3,4},{4,5},{5,6},{6,7},{7,8},{8,9},{9,10},{10,1... | collective-permute-start | bytes 196616 | tf_op jit(solution)/shard_map/ppermute | solution.py:14
  54.1 17.3 %collective-permute-start.7 = (f32[2,2,128,32]{2,3,1,0:T(8,128)S(1)}, f32[2,2,128,32]{2,3,1,0:T(8,128)S(1)}, u32[]{:S(2)}, u32[]{:S(2)}) collective-permute-start(f32[2,2,128,32]{2,3,1,0:T(8,128)S(1)} %scatter-add.35), channel_id=1, source_target_pairs={{1,0},{2,1},{3,2},{4,3},{5,4},{6,5},{7,6},{8,7},{9,8},{10,9},{11,1... | collective-permute-start | bytes 196616 | tf_op jit(solution)/shard_map/ppermute | solution.py:15
  56.7 14.0 %all-to-all-start.3 = ((f32[2,128,32]{1,0,2:T(2,128)}), f32[2,128,32]{1,0,2:T(2,128)S(1)}, u32[]{:S(2)}, u32[]{:S(2)}) async-start(f32[2,128,32]{1,0,2:T(2,128)} %copy.66), calls=%async_computation.3 | async-start | bytes 65536 | tf_op jit(solution)/shard_map/all_to_all | solution.py:102
  72.1 4.2 %copy-start.1 = (f32[2,128,32]{1,2,0:T(8,128)}, f32[2,128,32]{1,2,0:T(8,128)S(1)}, u32[]{:S(2)}) copy-start(f32[2,128,32]{1,2,0:T(8,128)S(1)} %get-tuple-element.340) | copy-start | bytes 98308
  72.8 146.7 %all-to-all-start.2 = ((f32[2,128,32]{1,0,2:T(2,128)}), f32[2,128,32]{1,0,2:T(2,128)S(1)}, u32[]{:S(2)}, u32[]{:S(2)}) async-start(f32[2,128,32]{1,0,2:T(2,128)} %copy.63), calls=%async_computation.2 | async-start | bytes 65536 | tf_op jit(solution)/shard_map/all_to_all | solution.py:101
where the time goes:
time: 224 us; the launch traced here: 220 us
  loops' own time  85 us (38%)
  local copies, waits for them, and re-layouts  67.3 us (30%)
  starting transfers between devices  47 us (21%)
  waiting for transfers between devices  10.6 us (5%)
  other arithmetic  5.48 us (2%)
  between operations  3.54 us (2%)
    another operation x1, loops' own time, lagged(): return lax.map(one_plane, lag_order)  85 us
    dynamic_update_slice x66, local copies, waits for them, and re-layouts, lagged(): return lax.map(one_plane, lag_order)  23 us
    dynamic_slice x33, local copies, waits for them, and re-layouts, lagged(): return lax.map(one_plane, lag_order)  19.9 us
    ppermute x4, starting transfers between devices, extended(): before = lax.ppermute(last, axis, up)  17.5 us
    dynamic_slice x132, local copies, waits for them, and re-layouts, one_plane(): moved_rcv = lax.dynamic_slice_in_dim(receiver, half + offset, cells_x, 2)  7.68 us
    all_to_all x1, starting transfers between devices, on_device(): lax.all_to_all(pair_old[0], 'wide', split_axis=2, concat_axis=0, tiled=True)  7.41 us
    all_to_all x1, starting transfers between devices, on_device(): lax.all_to_all(src_now, 'wide', split_axis=1, concat_axis=0, tiled=True)  7.39 us
    all_to_all x1, waiting for transfers between devices, on_device(): lax.all_to_all(pair_old[0], 'wide', split_axis=2, concat_axis=0, tiled=True)  6.59 us
  transfers between devices with their start and end apart: 12, of which 5 were waited for; matrix products, arithmetic and copies ran while one was open for 31% of the time, Pallas kernels for 0%

commit v1 on v0

--- a/solution.py
+++ b/solution.py
@@ -97,9 +97,13 @@
         pair_old, pair_now = (pair_now, pair_new)
         if step % 2 == 1:
             snaps.append((pair_now[0], pair_now[1]))
+    process_counts = lambda local_x: jnp.concatenate(
+        lax.all_to_all(jnp.stack(jnp.split(local_x, lax.axis_size("wide"), axis=2)), "wide", 0, 0),
+        axis=0,
+    )
     back_now, back_old = (
         lax.all_to_all(pair_now[0], "wide", split_axis=2, concat_axis=0, tiled=True),
-        lax.all_to_all(pair_old[0], "wide", split_axis=2, concat_axis=0, tiled=True),
+        process_counts(pair_old[0]),
     )
     src_next = jnp.transpose(back_now, (2, 0, 1))
     src_prior = jnp.transpose(back_old, (2, 0, 1))

time: 224 us -> 233 us (1.040)
  local copies, waits for them, and re-layouts: 67.3 us -> 76 us
    unnamed x12 -> x27, local copies, waits for them, and re-layouts: 2.84 us -> 11.5 us
  transfers between devices with their start and end apart: 12 -> 12, of which waited for: 5 -> 5; matrix products, arithmetic and copies ran while one was open for 31% -> 33% of each run, Pallas kernels for 0% -> 0%
where the time goes in v1:
time: 233 us; the launch traced here: 229 us
  loops' own time  85 us (36%)
  local copies, waits for them, and re-layouts  76 us (33%)
  starting transfers between devices  47 us (20%)
  waiting for transfers between devices  10.6 us (5%)
  other arithmetic  5.48 us (2%)
  between operations  3.55 us (2%)
    another operation x1, loops' own time, lagged(): return lax.map(one_plane, lag_order)  85 us
    dynamic_update_slice x66, local copies, waits for them, and re-layouts, lagged(): return lax.map(one_plane, lag_order)  23 us
    dynamic_slice x33, local copies, waits for them, and re-layouts, lagged(): return lax.map(one_plane, lag_order)  19.9 us
    ppermute x4, starting transfers between devices, extended(): before = lax.ppermute(last, axis, up)  17.5 us
    unnamed x27, local copies, waits for them, and re-layouts  11.5 us
    dynamic_slice x132, local copies, waits for them, and re-layouts, one_plane(): moved_rcv = lax.dynamic_slice_in_dim(receiver, half + offset, cells_x, 2)  7.68 us
    all_to_all x1, starting transfers between devices, on_device(): lax.all_to_all(jnp.stack(jnp.split(local_x, lax.axis_size('wide'), axis=2...  7.41 us
    all_to_all x1, starting transfers between devices, on_device(): lax.all_to_all(src_now, 'wide', split_axis=1, concat_axis=0, tiled=True)  7.39 us
  transfers between devices with their start and end apart: 12, of which 5 were waited for; matrix products, arithmetic and copies ran while one was open for 33% of the time, Pallas kernels for 0%

profile of v1, /device:TPU:0, one launch (start us, length us, event | category | flops | bytes accessed | tf_op | source)
XLA Modules:
  0.0 228.8 jit_solution(15906311758644785957)
XLA Ops:
  0.7 1.4 copy.55
  2.1 7.4 %all-to-all-start = ((f32[2,32,128]{2,0,1:T(2,128)}), f32[2,32,128]{2,0,1:T(2,128)S(1)}, u32[]{:S(2)}, u32[]{:S(2)}) async-start(f32[2,32,128]{2,0,1:T(2,128)} %copy.55), calls=%async_computation | async-start | bytes 65536 | tf_op jit(solution)/shard_map/all_to_all | solution.py:80
  9.5 0.8 slice_bitcast_fusion.8
  10.3 1.4 copy.57
  11.7 1.4 fusion.109
  13.0 0.6 compare_convert_fusion.1
  13.7 0.7 compare_convert_fusion.2
  14.4 1.4 fusion.108
  16.5 6.0 %all-to-all-start.1 = ((f32[2,32,128]{2,0,1:T(2,128)}), f32[2,32,128]{2,0,1:T(2,128)S(1)}, u32[]{:S(2)}, u32[]{:S(2)}) async-start(f32[2,32,128]{2,0,1:T(2,128)} %copy.57), calls=%async_computation.1 | async-start | bytes 65536 | tf_op jit(solution)/shard_map/all_to_all | solution.py:81
  22.5 0.8 pad_maximum_fusion.10
  23.3 2.3 %collective-permute-start = (f32[2,2,128,32]{2,3,1,0:T(8,128)S(1)}, f32[2,2,128,32]{2,3,1,0:T(8,128)S(1)}, u32[]{:S(2)}, u32[]{:S(2)}) collective-permute-start(f32[2,2,128,32]{2,3,1,0:T(8,128)S(1)} %pad_maximum_fusion.10), channel_id=1, source_target_pairs={{0,1},{1,2},{2,3},{3,4},{4,5},{5,6},{6,7},{7,8},{8,9},{9,10},{10,1... | collective-permute-start | bytes 196616 | tf_op jit(solution)/shard_map/ppermute | solution.py:14
  25.6 1.3 collective-permute-start.1
  26.9 0.7 compare_convert_fusion
  27.5 1.6 all-to-all-done.1
  29.1 0.7 collective-permute-done.1
  29.9 0.9 fusion.11
  31.3 4.8 %collective-permute-start.2 = (f32[2,2,128,32]{2,3,1,0:T(8,128)S(1)}, f32[2,2,128,32]{2,3,1,0:T(8,128)S(1)}, u32[]{:S(2)}, u32[]{:S(2)}) collective-permute-start(f32[2,2,128,32]{2,3,1,0:T(8,128)S(1)} %scatter-add.29), channel_id=1, source_target_pairs={{0,1},{1,2},{2,3},{3,4},{4,5},{5,6},{6,7},{7,8},{8,9},{9,10},{10,1... | collective-permute-start | bytes 196616 | tf_op jit(solution)/shard_map/ppermute | solution.py:14
  36.2 1.3 collective-permute-start.3
  38.1 1.2 collective-permute-done.3
  40.0 5.1 %collective-permute-start.4 = (f32[2,2,128,32]{2,3,1,0:T(8,128)S(1)}, f32[2,2,128,32]{2,3,1,0:T(8,128)S(1)}, u32[]{:S(2)}, u32[]{:S(2)}) collective-permute-start(f32[2,2,128,32]{2,3,1,0:T(8,128)S(1)} %scatter-add.31), channel_id=1, source_target_pairs={{0,1},{1,2},{2,3},{3,4},{4,5},{5,6},{6,7},{7,8},{8,9},{9,10},{10,1... | collective-permute-start | bytes 196616 | tf_op jit(solution)/shard_map/ppermute | solution.py:14
  45.1 1.3 collective-permute-start.5
  48.9 5.3 %collective-permute-start.6 = (f32[2,2,128,32]{2,3,1,0:T(8,128)S(1)}, f32[2,2,128,32]{2,3,1,0:T(8,128)S(1)}, u32[]{:S(2)}, u32[]{:S(2)}) collective-permute-start(f32[2,2,128,32]{2,3,1,0:T(8,128)S(1)} %scatter-add.35), channel_id=1, source_target_pairs={{0,1},{1,2},{2,3},{3,4},{4,5},{5,6},{6,7},{7,8},{8,9},{9,10},{10,1... | collective-permute-start | bytes 196616 | tf_op jit(solution)/shard_map/ppermute | solution.py:14
  54.1 1.3 collective-permute-start.7
  65.4 7.4 %all-to-all-start.3 = ((f32[16,2,128,2]{2,3,1,0:T(2,128)}), f32[16,2,128,2]{2,3,1,0:T(2,128)S(1)}, u32[]{:S(2)}, u32[]{:S(2)}) async-start(f32[16,2,128,2]{2,3,1,0:T(2,128)} %constant_dynamic-update-slice_fusion.1), calls=%async_computation.3 | async-start | bytes 65536 | tf_op jit(solution)/shard_map/all_to_all | solution.py:101
  72.8 6.6 %all-to-all-done.3 = f32[16,2,128,2]{2,3,1,0:T(2,128)S(1)} async-done(((f32[16,2,128,2]{2,3,1,0:T(2,128)}), f32[16,2,128,2]{2,3,1,0:T(2,128)S(1)}, u32[]{:S(2)}, u32[]{:S(2)}) %all-to-all-start.3) | async-done | bytes 32800 | tf_op jit(solution)/shard_map/all_to_all | solution.py:101
  80.7 0.6 copy.63
  81.4 3.5 %all-to-all-start.2 = ((f32[2,128,32]{1,0,2:T(2,128)}), f32[2,128,32]{1,0,2:T(2,128)S(1)}, u32[]{:S(2)}, u32[]{:S(2)}) async-start(f32[2,128,32]{1,0,2:T(2,128)} %copy.63), calls=%async_computation.2 | async-start | bytes 65536 | tf_op jit(solution)/shard_map/all_to_all | solution.py:105
  84.9 143.2 %while.23 = (s32[]{:T(128)}, f32[33,2,128,32]{2,3,1,0:T(8,128)}, s32[33]{0:T(128)S(1)}, f32[2,128,64]{1,2,0:T(8,128)S(1)}, f32[2,128,64]{1,2,0:T(8,128)S(1)}, /*...) while((s32[]{:T(128)}, f32[33,2,128,32]{2,3,1,0:T(8,128)}, ...), condition=%wide.region_1.2_spmd, body=%wide.region_0.1_spmd.sunk | while | flops 24586 | bytes 819957 | solution.py:58
  93.0 0.6 constant_dynamic-update-slice_fusion.18
  97.3 0.6 constant_dynamic-update-slice_fusion.18
  106.0 0.6 constant_dynamic-update-slice_fusion.18
  110.3 0.6 constant_dynamic-update-slice_fusion.18
  114.7 0.6 constant_dynamic-update-slice_fusion.18
  119.0 0.6 constant_dynamic-update-slice_fusion.18
  123.4 0.6 constant_dynamic-update-slice_fusion.18
  127.7 0.6 constant_dynamic-update-slice_fusion.18
  132.0 0.6 constant_dynamic-update-slice_fusion.18
  136.4 0.6 constant_dynamic-update-slice_fusion.18
  140.7 0.6 constant_dynamic-update-slice_fusion.18
  145.1 0.6 constant_dynamic-update-slice_fusion.18
  149.4 0.6 constant_dynamic-update-slice_fusion.18
  153.7 0.6 constant_dynamic-update-slice_fusion.18
  158.1 0.6 constant_dynamic-update-slice_fusion.18
  162.4 0.6 constant_dynamic-update-slice_fusion.18
  166.7 0.6 constant_dynamic-update-slice_fusion.18
  175.4 0.6 constant_dynamic-update-slice_fusion.18
  179.8 0.6 constant_dynamic-update-slice_fusion.18
  228.1 0.6 copy.65
  (373 shorter events, 59.8 us)
Async XLA Ops:
  0.6 38.7 %copy-start = (f32[2,128,32]{1,2,0:T(8,128)S(1)}, f32[2,128,32]{1,2,0:T(8,128)}, u32[]{:S(2)}) copy-start(f32[2,128,32]{1,2,0:T(8,128)} %param.30) | copy-start | bytes 98308
  0.6 30.2 %copy-start.2 = (f32[2,64,4]{1,2,0:T(4,128)S(1)}, f32[2,64,4]{1,2,0:T(4,128)}, u32[]{:S(2)}) copy-start(f32[2,64,4]{1,2,0:T(4,128)} %param.35) | copy-start | bytes 6148
  0.7 30.2 %copy-start.3 = (s32[2,64]{1,0:T(2,128)S(1)}, s32[2,64]{1,0:T(2,128)}, u32[]{:S(2)}) copy-start(s32[2,64]{1,0:T(2,128)} %param.36) | copy-start | bytes 1540
  2.1 14.4 %all-to-all-start = ((f32[2,32,128]{2,0,1:T(2,128)}), f32[2,32,128]{2,0,1:T(2,128)S(1)}, u32[]{:S(2)}, u32[]{:S(2)}) async-start(f32[2,32,128]{2,0,1:T(2,128)} %copy.55), calls=%async_computation | async-start | bytes 65536 | tf_op jit(solution)/shard_map/all_to_all | solution.py:80
  16.5 12.7 %all-to-all-start.1 = ((f32[2,32,128]{2,0,1:T(2,128)}), f32[2,32,128]{2,0,1:T(2,128)S(1)}, u32[]{:S(2)}, u32[]{:S(2)}) async-start(f32[2,32,128]{2,0,1:T(2,128)} %copy.57), calls=%async_computation.1 | async-start | bytes 65536 | tf_op jit(solution)/shard_map/all_to_all | solution.py:81
  23.3 5.9 %collective-permute-start = (f32[2,2,128,32]{2,3,1,0:T(8,128)S(1)}, f32[2,2,128,32]{2,3,1,0:T(8,128)S(1)}, u32[]{:S(2)}, u32[]{:S(2)}) collective-permute-start(f32[2,2,128,32]{2,3,1,0:T(8,128)S(1)} %pad_maximum_fusion.10), channel_id=1, source_target_pairs={{0,1},{1,2},{2,3},{3,4},{4,5},{5,6},{6,7},{7,8},{8,9},{9,10},{10,1... | collective-permute-start | bytes 196616 | tf_op jit(solution)/shard_map/ppermute | solution.py:14
  25.6 4.3 %collective-permute-start.1 = (f32[2,2,128,32]{2,3,1,0:T(8,128)S(1)}, f32[2,2,128,32]{2,3,1,0:T(8,128)S(1)}, u32[]{:S(2)}, u32[]{:S(2)}) collective-permute-start(f32[2,2,128,32]{2,3,1,0:T(8,128)S(1)} %pad_maximum_fusion.10), channel_id=1, source_target_pairs={{1,0},{2,1},{3,2},{4,3},{5,4},{6,5},{7,6},{8,7},{9,8},{10,9},{11,1... | collective-permute-start | bytes 196616 | tf_op jit(solution)/shard_map/ppermute | solution.py:15
  31.3 6.8 %collective-permute-start.2 = (f32[2,2,128,32]{2,3,1,0:T(8,128)S(1)}, f32[2,2,128,32]{2,3,1,0:T(8,128)S(1)}, u32[]{:S(2)}, u32[]{:S(2)}) collective-permute-start(f32[2,2,128,32]{2,3,1,0:T(8,128)S(1)} %scatter-add.29), channel_id=1, source_target_pairs={{0,1},{1,2},{2,3},{3,4},{4,5},{5,6},{6,7},{7,8},{8,9},{9,10},{10,1... | collective-permute-start | bytes 196616 | tf_op jit(solution)/shard_map/ppermute | solution.py:14
  36.2 3.1 %collective-permute-start.3 = (f32[2,2,128,32]{2,3,1,0:T(8,128)S(1)}, f32[2,2,128,32]{2,3,1,0:T(8,128)S(1)}, u32[]{:S(2)}, u32[]{:S(2)}) collective-permute-start(f32[2,2,128,32]{2,3,1,0:T(8,128)S(1)} %scatter-add.29), channel_id=1, source_target_pairs={{1,0},{2,1},{3,2},{4,3},{5,4},{6,5},{7,6},{8,7},{9,8},{10,9},{11,1... | collective-permute-start | bytes 196616 | tf_op jit(solution)/shard_map/ppermute | solution.py:15
  40.0 7.7 %collective-permute-start.4 = (f32[2,2,128,32]{2,3,1,0:T(8,128)S(1)}, f32[2,2,128,32]{2,3,1,0:T(8,128)S(1)}, u32[]{:S(2)}, u32[]{:S(2)}) collective-permute-start(f32[2,2,128,32]{2,3,1,0:T(8,128)S(1)} %scatter-add.31), channel_id=1, source_target_pairs={{0,1},{1,2},{2,3},{3,4},{4,5},{5,6},{6,7},{7,8},{8,9},{9,10},{10,1... | collective-permute-start | bytes 196616 | tf_op jit(solution)/shard_map/ppermute | solution.py:14
  45.1 3.1 %collective-permute-start.5 = (f32[2,2,128,32]{2,3,1,0:T(8,128)S(1)}, f32[2,2,128,32]{2,3,1,0:T(8,128)S(1)}, u32[]{:S(2)}, u32[]{:S(2)}) collective-permute-start(f32[2,2,128,32]{2,3,1,0:T(8,128)S(1)} %scatter-add.31), channel_id=1, source_target_pairs={{1,0},{2,1},{3,2},{4,3},{5,4},{6,5},{7,6},{8,7},{9,8},{10,9},{11,1... | collective-permute-start | bytes 196616 | tf_op jit(solution)/shard_map/ppermute | solution.py:15
  48.4 36.5 %copy-start.4 = (s32[33]{0:T(128)S(1)}, s32[33]{0:T(128)}, u32[]{:S(2)}) copy-start(s32[33]{0:T(128)} %param.37) | copy-start | bytes 400
  48.9 31.2 %collective-permute-start.6 = (f32[2,2,128,32]{2,3,1,0:T(8,128)S(1)}, f32[2,2,128,32]{2,3,1,0:T(8,128)S(1)}, u32[]{:S(2)}, u32[]{:S(2)}) collective-permute-start(f32[2,2,128,32]{2,3,1,0:T(8,128)S(1)} %scatter-add.35), channel_id=1, source_target_pairs={{0,1},{1,2},{2,3},{3,4},{4,5},{5,6},{6,7},{7,8},{8,9},{9,10},{10,1... | collective-permute-start | bytes 196616 | tf_op jit(solution)/shard_map/ppermute | solution.py:14
  54.1 25.9 %collective-permute-start.7 = (f32[2,2,128,32]{2,3,1,0:T(8,128)S(1)}, f32[2,2,128,32]{2,3,1,0:T(8,128)S(1)}, u32[]{:S(2)}, u32[]{:S(2)}) collective-permute-start(f32[2,2,128,32]{2,3,1,0:T(8,128)S(1)} %scatter-add.35), channel_id=1, source_target_pairs={{1,0},{2,1},{3,2},{4,3},{5,4},{6,5},{7,6},{8,7},{9,8},{10,9},{11,1... | collective-permute-start | bytes 196616 | tf_op jit(solution)/shard_map/ppermute | solution.py:15
  65.4 14.0 %all-to-all-start.3 = ((f32[16,2,128,2]{2,3,1,0:T(2,128)}), f32[16,2,128,2]{2,3,1,0:T(2,128)S(1)}, u32[]{:S(2)}, u32[]{:S(2)}) async-start(f32[16,2,128,2]{2,3,1,0:T(2,128)} %constant_dynamic-update-slice_fusion.1), calls=%async_computation.3 | async-start | bytes 65536 | tf_op jit(solution)/shard_map/all_to_all | solution.py:101
  80.7 4.2 %copy-start.1 = (f32[2,128,32]{1,2,0:T(8,128)}, f32[2,128,32]{1,2,0:T(8,128)S(1)}, u32[]{:S(2)}) copy-start(f32[2,128,32]{1,2,0:T(8,128)S(1)} %get-tuple-element.340) | copy-start | bytes 98308
  81.4 146.7 %all-to-all-start.2 = ((f32[2,128,32]{1,0,2:T(2,128)}), f32[2,128,32]{1,0,2:T(2,128)S(1)}, u32[]{:S(2)}, u32[]{:S(2)}) async-start(f32[2,128,32]{1,0,2:T(2,128)} %copy.63), calls=%async_computation.2 | async-start | bytes 65536 | tf_op jit(solution)/shard_map/all_to_all | solution.py:105
